TPU v7x, 256 devices: a whole 4x4x8 slice. The times are simulated.
256 devices in a mesh: space: 32 (over x, z_hi, y), ens: 8 (over z_lo, core).
Axes of the slice: x: 4, y: 4, z: 8 (z_hi: 2, z_lo: 4; z = z_hi * 4 + z_lo), core: 2. Of those that a mesh axis runs over, the one named last changes fastest.
Arguments:
- outlook_array: bfloat16 [1536, 49152], P('ens', 'space'), may hold values from -57 to 57
- earlier_location_basis: bfloat16 [49152, 256], P('space'), may hold values from -4 to 4
- earlier_ensemble_basis: float32 [48, 16], replicated, may hold values from -4 to 4
- earlier_height_basis: float32 [32, 16], replicated, may hold values from -4 to 4
Outputs:
- spatial_factor: float32 [49152, 256], P(('space', 'ens'))
- member_factor: float32 [48, 16], replicated
- level_factor: float32 [32, 16], replicated
All inputs are finite; a program needn't handle non-finite values.
Results may differ from a plain program's by a relative error of at most 0.0075.
The roundings to bfloat16 on the way count: a program that leaves them out, or rounds other values in their place, can miss the bound.
Values may be sent and summed in bfloat16 or wider, within the bound.
A program may use at most 64 MiB of HBM per device.

v0:
```python
import jax
import jax.numpy as jnp
from jax import lax
from jax.sharding import PartitionSpec as P

MEMBERS = 48
LEVELS = 32
PASSES = 3
highest = lax.Precision.HIGHEST


def inner_gram(image_rows):
    return lax.dot_general(
        image_rows,
        image_rows,
        (((0,), (0,)), ((), ())),
        precision=highest,
        preferred_element_type=jnp.float32,
    )


def solve_right(lower_factor, image_rows):
    return lax.linalg.triangular_solve(
        lower_factor, image_rows, left_side=False, lower=True, transpose_a=True
    )


def refine(gram_matrix, previous, row_count):
    image_rows = jnp.dot(
        gram_matrix, previous, precision=highest, preferred_element_type=jnp.float32
    )
    lower_factor = jnp.linalg.cholesky(inner_gram(image_rows) / row_count)
    return solve_right(lower_factor, image_rows)


def factor_grams(final_band_lines):
    by_level = final_band_lines.reshape(LEVELS, -1)
    level_gram = jnp.dot(by_level, by_level.T, preferred_element_type=jnp.float32)
    by_member = (
        final_band_lines.reshape(LEVELS, MEMBERS, -1).transpose(1, 0, 2).reshape(MEMBERS, -1)
    )
    member_gram = jnp.dot(by_member, by_member.T, preferred_element_type=jnp.float32)
    return (member_gram, level_gram)


def spatial_step(ensemble_variance, grid_total):
    gram_total = lax.psum(inner_gram(ensemble_variance), ("space", "ens")) / grid_total
    return solve_right(jnp.linalg.cholesky(gram_total), ensemble_variance)


def project(vertical_cells, location_basis_matrix):
    row_share = lax.psum_scatter(
        jnp.dot(vertical_cells, location_basis_matrix, preferred_element_type=jnp.float32),
        "ens",
        scatter_dimension=0,
        tiled=True,
    )
    row_share = lax.psum(row_share, "space")
    return lax.all_gather(row_share.astype(jnp.bfloat16), "ens", axis=0, tiled=True)


def on_device(outlook_array, earlier_location_basis, earlier_ensemble_basis, earlier_height_basis):
    ens_count = lax.axis_size("ens")
    grid_dev = earlier_location_basis.shape[0]
    sub_rows = grid_dev // ens_count
    grid_total = grid_dev * lax.axis_size("space")
    factor = None
    final_band_lines = None
    vertical_cells = lax.all_to_all(outlook_array, "ens", split_axis=1, concat_axis=0, tiled=True)
    first_row = lax.axis_index("ens") * sub_rows
    location_basis_matrix = lax.dynamic_slice_in_dim(earlier_location_basis, first_row, sub_rows, 0)
    for pass_index in range(PASSES + 1):
        final_band_lines = project(vertical_cells, location_basis_matrix)
        if pass_index < PASSES:
            ensemble_variance = lax.dot_general(
                vertical_cells,
                final_band_lines,
                (((0,), (0,)), ((), ())),
                preferred_element_type=jnp.float32,
            )
            factor = spatial_step(ensemble_variance, grid_total)
            location_basis_matrix = factor.astype(jnp.bfloat16)
    member_gram, level_gram = factor_grams(final_band_lines)
    return (
        factor,
        refine(member_gram, earlier_ensemble_basis, MEMBERS),
        refine(level_gram, earlier_height_basis, LEVELS),
    )


def solution(mesh):
    in_specs = (P("ens", "space"), P("space", None), P(), P())
    out_specs = (P(("space", "ens"), None), P(), P())
    return jax.shard_map(
        on_device, mesh=mesh, in_specs=in_specs, out_specs=out_specs, check_vma=False
    )
```

profile of v0, /device:TPU:1, one launch (start us, length us, event | category | flops | bytes accessed | tf_op | source)
XLA Modules:
  0.0 2115.9 jit_solution(5704616628953250704)
XLA Ops:
  7.2 2.3 copy.46
  9.5 7.4 all-to-all-start
  16.9 20.0 all-to-all-done
  37.3 0.7 all_to_all.17
  38.4 1.6 copy.67
  40.1 37.7 %reduce-scatter.13.cloned.1.call-done = f32[192,256]{1,0:T(8,128)} async-done(((f32[1536,256]{1,0:T(8,128)}), f32[192,256]{1,0:T(8,128)}) %reduce-scatter.13.cloned.1.call-update) | async-done | bytes 196624 | tf_op jit(solution)/shard_map/reduce_scatter | solution.py:52
  77.8 198.7 %all-reduce.14 = bf16[192,256]{1,0:T(8,128)(2,1)S(1)} all-reduce(f32[192,256]{1,0:T(8,128)} %reduce-scatter.13.cloned.1.call-done), channel_id=1, replica_groups=mesh['space'=32,'ens'=8] {'space'}, use_global_device_ids=true, to_apply=%region_1.0 | all-reduce | flops 49152 | bytes 294912 | tf_op jit(solution)/shard_map/psum | solution.py:58
  276.4 44.7 %all_gather.12 = bf16[1536,256]{1,0:T(8,128)(2,1)S(1)} all-gather(bf16[192,256]{1,0:T(8,128)(2,1)S(1)} %all-reduce.14), channel_id=1, replica_groups=mesh['space'=32,'ens'=8] {'ens'}, dimensions={0}, use_global_device_ids=true | all-gather | bytes 884736 | tf_op jit(solution)/shard_map/all_gather | solution.py:59
  321.4 1.4 fusion.48
  323.4 243.8 %all-reduce.9.cloned.1.call-done = f32[256,256]{0,1:T(8,128)} async-done(((f32[256,256]{0,1:T(8,128)}), f32[256,256]{0,1:T(8,128)}) %all-reduce.9.cloned.1.call-update) | async-done | bytes 262160 | tf_op jit(solution)/shard_map/psum | solution.py:47
  567.2 1.0 broadcast_multiply_fusion.2
  568.3 1.0 fusion.2
  569.3 11.7 cholesky.214
  581.1 9.8 custom-call.25
  591.4 11.7 cholesky.231
  603.1 0.7 compare_reduce_fusion.6
  605.3 4.3 while.6
  606.1 1.4 bitcast_dynamic-update-slice_fusion.6
  608.2 1.4 bitcast_dynamic-update-slice_fusion.6
  609.6 19.7 custom-call.26
  630.5 1.6 copy.69
  632.2 37.2 %reduce-scatter.15.cloned.1.call-done = f32[192,256]{1,0:T(8,128)} async-done(((f32[1536,256]{1,0:T(8,128)}), f32[192,256]{1,0:T(8,128)}) %reduce-scatter.15.cloned.1.call-update) | async-done | bytes 196624 | tf_op jit(solution)/shard_map/reduce_scatter | solution.py:52
  669.3 198.6 %all-reduce.15 = bf16[192,256]{1,0:T(8,128)(2,1)S(1)} all-reduce(f32[192,256]{1,0:T(8,128)} %reduce-scatter.15.cloned.1.call-done), channel_id=1, replica_groups=mesh['space'=32,'ens'=8] {'space'}, use_global_device_ids=true, to_apply=%region_8.11 | all-reduce | flops 49152 | bytes 294912 | tf_op jit(solution)/shard_map/psum | solution.py:58
  867.9 44.7 %all_gather.13 = bf16[1536,256]{1,0:T(8,128)(2,1)S(1)} all-gather(bf16[192,256]{1,0:T(8,128)(2,1)S(1)} %all-reduce.15), channel_id=1, replica_groups=mesh['space'=32,'ens'=8] {'ens'}, dimensions={0}, use_global_device_ids=true | all-gather | bytes 884736 | tf_op jit(solution)/shard_map/all_gather | solution.py:59
  912.9 1.4 fusion.49
  914.4 244.5 %all-reduce.11.cloned.1.call-done = f32[256,256]{0,1:T(8,128)} async-done(((f32[256,256]{0,1:T(8,128)}), f32[256,256]{0,1:T(8,128)}) %all-reduce.11.cloned.1.call-update) | async-done | bytes 262160 | tf_op jit(solution)/shard_map/psum | solution.py:47
  1158.9 1.0 broadcast_multiply_fusion.1
  1160.0 1.0 fusion.1
  1161.1 11.7 cholesky.248
  1172.8 9.8 custom-call.27
  1183.1 11.7 cholesky.265
  1194.9 0.7 compare_reduce_fusion.4
  1197.6 4.5 while.7
  1198.6 1.4 bitcast_dynamic-update-slice_fusion.7
  1200.7 1.4 bitcast_dynamic-update-slice_fusion.7
  1202.1 19.7 custom-call.28
  1223.0 1.6 copy.71
  1224.7 37.2 %reduce-scatter.17.cloned.1.call-done = f32[192,256]{1,0:T(8,128)} async-done(((f32[1536,256]{1,0:T(8,128)}), f32[192,256]{1,0:T(8,128)}) %reduce-scatter.17.cloned.1.call-update) | async-done | bytes 196624 | tf_op jit(solution)/shard_map/reduce_scatter | solution.py:52
  1261.9 198.8 %all-reduce.16 = bf16[192,256]{1,0:T(8,128)(2,1)S(1)} all-reduce(f32[192,256]{1,0:T(8,128)} %reduce-scatter.17.cloned.1.call-done), channel_id=1, replica_groups=mesh['space'=32,'ens'=8] {'space'}, use_global_device_ids=true, to_apply=%region_11.14 | all-reduce | flops 49152 | bytes 294912 | tf_op jit(solution)/shard_map/psum | solution.py:58
  1460.7 44.6 %all_gather.14 = bf16[1536,256]{1,0:T(8,128)(2,1)S(1)} all-gather(bf16[192,256]{1,0:T(8,128)(2,1)S(1)} %all-reduce.16), channel_id=1, replica_groups=mesh['space'=32,'ens'=8] {'ens'}, dimensions={0}, use_global_device_ids=true | all-gather | bytes 884736 | tf_op jit(solution)/shard_map/all_gather | solution.py:59
  1505.7 1.4 fusion.50
  1507.1 244.3 %all-reduce.13.cloned.1.call-done = f32[256,256]{0,1:T(8,128)} async-done(((f32[256,256]{0,1:T(8,128)}), f32[256,256]{0,1:T(8,128)}) %all-reduce.13.cloned.1.call-update) | async-done | bytes 262160 | tf_op jit(solution)/shard_map/psum | solution.py:47
  1751.4 1.0 broadcast_multiply_fusion
  1752.5 1.0 fusion
  1753.5 11.7 cholesky.282
  1765.3 9.8 custom-call.29
  1775.6 11.7 cholesky.299
  1790.0 4.2 while.8
  1790.8 1.4 bitcast_dynamic-update-slice_fusion.8
  1792.8 1.4 bitcast_dynamic-update-slice_fusion.8
  1794.2 19.7 custom-call.30
  1815.0 1.6 copy.73
  1816.7 37.2 %reduce-scatter.19.cloned.1.call-done = f32[192,256]{1,0:T(8,128)} async-done(((f32[1536,256]{1,0:T(8,128)}), f32[192,256]{1,0:T(8,128)}) %reduce-scatter.19.cloned.1.call-update) | async-done | bytes 196624 | tf_op jit(solution)/shard_map/reduce_scatter | solution.py:52
  1853.9 198.8 %all-reduce.17 = bf16[192,256]{1,0:T(8,128)(2,1)S(1)} all-reduce(f32[192,256]{1,0:T(8,128)} %reduce-scatter.19.cloned.1.call-done), channel_id=1, replica_groups=mesh['space'=32,'ens'=8] {'space'}, use_global_device_ids=true, to_apply=%region_14.17 | all-reduce | flops 49152 | bytes 294912 | tf_op jit(solution)/shard_map/psum | solution.py:58
  2052.7 44.6 %all_gather.15 = bf16[1536,256]{1,0:T(8,128)(2,1)S(1)} all-gather(bf16[192,256]{1,0:T(8,128)(2,1)S(1)} %all-reduce.17), channel_id=1, replica_groups=mesh['space'=32,'ens'=8] {'ens'}, dimensions={0}, use_global_device_ids=true | all-gather | bytes 884736 | tf_op jit(solution)/shard_map/all_gather | solution.py:59
  2098.4 1.5 cholesky.325
  2099.9 0.6 compare_reduce_fusion
  2100.6 0.6 fusion.35
  2101.2 1.2 custom-call.20
  2102.5 0.8 fusion.36
  2104.0 1.5 cholesky.314
  2106.2 0.6 fusion.34
  2106.8 1.2 custom-call.19
  2108.0 0.8 fusion.39
  (98 shorter events, 16.4 us)
Async XLA Ops:
  7.2 30.8 %copy-start = (bf16[1536,256]{1,0:T(8,128)(2,1)S(1)}, bf16[1536,256]{1,0:T(8,128)(2,1)}, u32[]{:S(2)}) copy-start(bf16[1536,256]{1,0:T(8,128)(2,1)} %param.9) | copy-start | bytes 2359300
  9.5 27.4 %all-to-all-start = ((bf16[192,8,192]{0,2,1:T(8,128)(2,1)}), bf16[192,8,192]{0,2,1:T(8,128)(2,1)S(1)}, u32[]{:S(2)}, u32[]{:S(2)}) async-start(bf16[192,8,192]{0,2,1:T(8,128)(2,1)} %bitcast), calls=%async_computation | async-start | bytes 1572864 | tf_op jit(solution)/shard_map/all_to_all | solution.py:69
  16.9 60.9 %reduce-scatter.13.cloned.1.call-start = ((), (), s32[]{:S(2)}) async-start(), calls=%async_computation.8 | async-start | bytes 1769472 | tf_op jit(solution)/shard_map/reduce_scatter | solution.py:52
  40.0 527.2 %all-reduce.9.cloned.1.call-start = ((), (), s32[]{:S(2)}) async-start(), calls=%async_computation.5 | async-start | bytes 524288 | tf_op jit(solution)/shard_map/psum | solution.py:47
  322.8 346.5 %reduce-scatter.15.cloned.1.call-start = ((), (), s32[]{:S(2)}) async-start(), calls=%async_computation.9 | async-start | bytes 1769472 | tf_op jit(solution)/shard_map/reduce_scatter | solution.py:52
  632.1 526.8 %all-reduce.11.cloned.1.call-start = ((), (), s32[]{:S(2)}) async-start(), calls=%async_computation.6 | async-start | bytes 524288 | tf_op jit(solution)/shard_map/psum | solution.py:47
  914.3 347.6 %reduce-scatter.17.cloned.1.call-start = ((), (), s32[]{:S(2)}) async-start(), calls=%async_computation.10 | async-start | bytes 1769472 | tf_op jit(solution)/shard_map/reduce_scatter | solution.py:52
  1224.6 526.8 %all-reduce.13.cloned.1.call-start = ((), (), s32[]{:S(2)}) async-start(), calls=%async_computation.7 | async-start | bytes 524288 | tf_op jit(solution)/shard_map/psum | solution.py:47
  1507.1 346.9 %reduce-scatter.19.cloned.1.call-start = ((), (), s32[]{:S(2)}) async-start(), calls=%async_computation.11 | async-start | bytes 1769472 | tf_op jit(solution)/shard_map/reduce_scatter | solution.py:52
  1814.6 2.0 copy-start.1
  2097.3 0.7 copy-start.3
  2097.7 5.9 copy-start.2
Sparse Core Ops, SparseCore 0:
  40.1 37.5 reduce-scatter.12
  323.0 244.1 all-reduce.8
  632.2 37.0 reduce-scatter.14
  914.5 244.4 all-reduce.10
  1224.8 37.0 reduce-scatter.16
  1507.2 244.1 all-reduce.12
  1816.8 37.0 reduce-scatter.18
where the time goes:
time: 2120 us
  blocking collectives  973 us (46%)
  waiting for transfers between devices  902 us (43%)
  other arithmetic  176 us (8%)
  local copies, waits for them, and re-layouts  23.1 us (1%)
    psum x4, blocking collectives, project(): row_share = lax.psum(row_share, 'space')  795 us
    psum x3, waiting for transfers between devices, spatial_step(): lax.psum(inner_gram(ensemble_variance), ('space', 'ens')) / grid_total  733 us
    all_gather x4, blocking collectives, project(): lax.all_gather(row_share.astype(jnp.bfloat16), 'ens', axis=0, tiled=True)  179 us
    reduce_scatter x4, waiting for transfers between devices, project(): lax.psum_scatter(jnp.dot(vertical_cells, location_basis_matrix, preferred...  149 us
    another operation x20, other arithmetic, spatial_step(): return solve_right(jnp.linalg.cholesky(gram_total), ensemble_variance)  103 us
    another operation x12, other arithmetic, solve_right(): lax.linalg.triangular_solve(lower_factor, image_rows, left_side=False, lo...  62.9 us
  transfers between devices with their start and end apart: 8, of which 8 were waited for; matrix products, arithmetic and copies ran while one was open for 0% of the time, Pallas kernels for 0%

commit v1 on v0

--- a/solution.py
+++ b/solution.py
@@ -7,6 +7,12 @@
 LEVELS = 32
 PASSES = 3
 highest = lax.Precision.HIGHEST
+
+
+def point_tracks(u, group_axis):
+    small = jax.lax.all_gather(u, group_axis)
+    then = jnp.sum(small, 0)
+    return then
 
 
 def inner_gram(image_rows):
@@ -55,7 +61,7 @@
         scatter_dimension=0,
         tiled=True,
     )
-    row_share = lax.psum(row_share, "space")
+    row_share = point_tracks(row_share, "space")
     return lax.all_gather(row_share.astype(jnp.bfloat16), "ens", axis=0, tiled=True)
 
 

time: 2120 us -> 1780 us (0.84)
  blocking collectives: 973 us -> 69.7 us
  waiting for transfers between devices: 902 us -> 1450 us
    psum x4 -> x0, blocking collectives: 795 us -> none  [project(): row_share = lax.psum(row_share, 'space')]
    all_gather x0 -> x4, waiting for transfers between devices: none -> 542 us  [point_tracks(): small = jax.lax.all_gather(u, group_axis)]
    all_gather x4, blocking collectives: 179 us -> 69.7 us  [project(): lax.all_gather(row_share.astype(jnp.bfloat16), 'ens', axis=0, tiled=True)]
  transfers between devices with their start and end apart: 8 -> 12, of which waited for: 8 -> 12; matrix products, arithmetic and copies ran while one was open for 0% -> 0% of each run, Pallas kernels for 0% -> 0%
where the time goes in v1:
time: 1780 us; the launch traced here: 1770 us
  waiting for transfers between devices  1450 us (81%)
  other arithmetic  189 us (11%)
  blocking collectives  69.7 us (4%)
  local copies, waits for them, and re-layouts  23.1 us (1%)
  between operations  18.5 us (1%)
    psum x3, waiting for transfers between devices, spatial_step(): lax.psum(inner_gram(ensemble_variance), ('space', 'ens')) / grid_total  740 us
    all_gather x4, waiting for transfers between devices, point_tracks(): small = jax.lax.all_gather(u, group_axis)  542 us
    reduce_scatter x4, waiting for transfers between devices, project(): lax.psum_scatter(jnp.dot(vertical_cells, location_basis_matrix, preferred...  149 us
    another operation x20, other arithmetic, spatial_step(): return solve_right(jnp.linalg.cholesky(gram_total), ensemble_variance)  103 us
    all_gather x4, blocking collectives, project(): lax.all_gather(row_share.astype(jnp.bfloat16), 'ens', axis=0, tiled=True)  69.7 us
    another operation x12, other arithmetic, solve_right(): lax.linalg.triangular_solve(lower_factor, image_rows, left_side=False, lo...  62.9 us
  transfers between devices with their start and end apart: 12, of which 12 were waited for; matrix products, arithmetic and copies ran while one was open for 0% of the time, Pallas kernels for 0%

profile of v1, /device:TPU:1, one launch (start us, length us, event | category | flops | bytes accessed | tf_op | source)
XLA Modules:
  0.0 1774.1 jit_solution(1929490882614571627)
XLA Ops:
  7.2 2.3 copy.32
  9.5 7.4 all-to-all-start
  16.9 20.0 %all-to-all-done = bf16[192,8,192]{0,2,1:T(8,128)(2,1)S(1)} async-done(((bf16[192,8,192]{0,2,1:T(8,128)(2,1)}), bf16[192,8,192]{0,2,1:T(8,128)(2,1)S(1)}, u32[]{:S(2)}, u32[]{:S(2)}) %all-to-all-start) | async-done | bytes 589856 | tf_op jit(solution)/shard_map/all_to_all | solution.py:75
  38.4 1.6 copy.53
  40.1 37.7 %reduce-scatter.13.cloned.1.call-done = f32[192,256]{1,0:T(8,128)} async-done(((f32[1536,256]{1,0:T(8,128)}), f32[192,256]{1,0:T(8,128)}) %reduce-scatter.13.cloned.1.call-update) | async-done | bytes 196624 | tf_op jit(solution)/shard_map/reduce_scatter | solution.py:58
  77.8 135.7 %all-gather.9.cloned.1.call-done = f32[6144,256]{1,0:T(8,128)} async-done(((f32[192,256]{1,0:T(8,128)}), f32[6144,256]{1,0:T(8,128)}) %all-gather.9.cloned.1.call-update) | async-done | bytes 6291472 | tf_op jit(solution)/shard_map/all_gather | solution.py:13
  213.5 3.2 reduce_sum.36
  216.7 17.4 all_gather.38
  234.5 1.4 fusion.48
  236.1 246.3 %all-reduce.5.cloned.1.call-done = f32[256,256]{0,1:T(8,128)} async-done(((f32[256,256]{0,1:T(8,128)}), f32[256,256]{0,1:T(8,128)}) %all-reduce.5.cloned.1.call-update) | async-done | bytes 262160 | tf_op jit(solution)/shard_map/psum | solution.py:53
  482.4 1.0 broadcast_multiply_fusion.2
  483.5 1.0 fusion.2
  484.6 11.7 cholesky.214
  496.3 9.8 custom-call.25
  506.6 11.7 cholesky.231
  518.4 0.7 compare_reduce_fusion.6
  520.6 4.5 while.6
  521.6 1.4 bitcast_dynamic-update-slice_fusion.6
  523.6 1.4 bitcast_dynamic-update-slice_fusion.6
  525.1 19.7 %custom-call.26 = f32[2,128,128]{1,2,0:T(8,128)S(1)} custom-call(f32[2,128,128]{2,1,0:T(8,128)S(1)} %get-tuple-element.26), custom_call_target="InvertDiagBlocksLowerTriangular" | custom-call | tf_op jit(solution)/shard_map/triangular_solve/custom-call.4 | solution.py:29
  545.9 1.6 copy.55
  547.6 37.2 %reduce-scatter.15.cloned.1.call-done = f32[192,256]{1,0:T(8,128)} async-done(((f32[1536,256]{1,0:T(8,128)}), f32[192,256]{1,0:T(8,128)}) %reduce-scatter.15.cloned.1.call-update) | async-done | bytes 196624 | tf_op jit(solution)/shard_map/reduce_scatter | solution.py:58
  584.9 135.4 %all-gather.11.cloned.1.call-done = f32[6144,256]{1,0:T(8,128)} async-done(((f32[192,256]{1,0:T(8,128)}), f32[6144,256]{1,0:T(8,128)}) %all-gather.11.cloned.1.call-update) | async-done | bytes 6291472 | tf_op jit(solution)/shard_map/all_gather | solution.py:13
  720.4 3.2 reduce_sum.37
  723.5 17.4 all_gather.41
  741.3 1.4 fusion.49
  742.7 246.7 %all-reduce.7.cloned.1.call-done = f32[256,256]{0,1:T(8,128)} async-done(((f32[256,256]{0,1:T(8,128)}), f32[256,256]{0,1:T(8,128)}) %all-reduce.7.cloned.1.call-update) | async-done | bytes 262160 | tf_op jit(solution)/shard_map/psum | solution.py:53
  989.5 1.0 broadcast_multiply_fusion.1
  990.6 1.0 fusion.1
  991.6 11.7 cholesky.248
  1003.4 9.8 custom-call.27
  1013.7 11.7 cholesky.265
  1025.4 0.7 compare_reduce_fusion.4
  1028.2 4.3 while.7
  1029.0 1.4 bitcast_dynamic-update-slice_fusion.7
  1031.0 1.4 bitcast_dynamic-update-slice_fusion.7
  1032.4 19.7 %custom-call.28 = f32[2,128,128]{1,2,0:T(8,128)S(1)} custom-call(f32[2,128,128]{2,1,0:T(8,128)S(1)} %get-tuple-element.27), custom_call_target="InvertDiagBlocksLowerTriangular" | custom-call | tf_op jit(solution)/shard_map/triangular_solve/custom-call.4 | solution.py:29
  1053.3 1.6 copy.57
  1055.0 37.2 %reduce-scatter.17.cloned.1.call-done = f32[192,256]{1,0:T(8,128)} async-done(((f32[1536,256]{1,0:T(8,128)}), f32[192,256]{1,0:T(8,128)}) %reduce-scatter.17.cloned.1.call-update) | async-done | bytes 196624 | tf_op jit(solution)/shard_map/reduce_scatter | solution.py:58
  1092.3 135.6 %all-gather.13.cloned.1.call-done = f32[6144,256]{1,0:T(8,128)} async-done(((f32[192,256]{1,0:T(8,128)}), f32[6144,256]{1,0:T(8,128)}) %all-gather.13.cloned.1.call-update) | async-done | bytes 6291472 | tf_op jit(solution)/shard_map/all_gather | solution.py:13
  1227.9 3.2 reduce_sum.38
  1231.0 17.4 all_gather.44
  1248.8 1.4 fusion.50
  1250.3 246.7 %all-reduce.9.cloned.1.call-done = f32[256,256]{0,1:T(8,128)} async-done(((f32[256,256]{0,1:T(8,128)}), f32[256,256]{0,1:T(8,128)}) %all-reduce.9.cloned.1.call-update) | async-done | bytes 262160 | tf_op jit(solution)/shard_map/psum | solution.py:53
  1497.0 1.0 broadcast_multiply_fusion
  1498.1 1.0 fusion
  1499.1 11.7 cholesky.282
  1510.9 9.8 custom-call.29
  1521.2 11.7 cholesky.299
  1535.5 4.2 while.8
  1536.4 1.4 bitcast_dynamic-update-slice_fusion.8
  1538.4 1.4 bitcast_dynamic-update-slice_fusion.8
  1539.8 19.7 %custom-call.30 = f32[2,128,128]{1,2,0:T(8,128)S(1)} custom-call(f32[2,128,128]{2,1,0:T(8,128)S(1)} %get-tuple-element.28), custom_call_target="InvertDiagBlocksLowerTriangular" | custom-call | tf_op jit(solution)/shard_map/triangular_solve/custom-call.4 | solution.py:29
  1560.6 1.6 copy.59
  1562.3 37.2 %reduce-scatter.19.cloned.1.call-done = f32[192,256]{1,0:T(8,128)} async-done(((f32[1536,256]{1,0:T(8,128)}), f32[192,256]{1,0:T(8,128)}) %reduce-scatter.19.cloned.1.call-update) | async-done | bytes 196624 | tf_op jit(solution)/shard_map/reduce_scatter | solution.py:58
  1599.6 135.6 %all-gather.15.cloned.1.call-done = f32[6144,256]{1,0:T(8,128)} async-done(((f32[192,256]{1,0:T(8,128)}), f32[6144,256]{1,0:T(8,128)}) %all-gather.15.cloned.1.call-update) | async-done | bytes 6291472 | tf_op jit(solution)/shard_map/all_gather | solution.py:13
  1735.2 3.2 reduce_sum.39
  1738.4 17.4 all_gather.47
  1756.9 1.5 cholesky.325
  1759.7 1.2 custom-call.20
  1760.9 0.8 fusion.36
  1762.5 1.5 cholesky.314
  1765.3 1.2 custom-call.19
  1766.5 0.8 fusion.39
  (110 shorter events, 18.9 us)
Async XLA Ops:
  7.2 30.8 %copy-start = (bf16[1536,256]{1,0:T(8,128)(2,1)S(1)}, bf16[1536,256]{1,0:T(8,128)(2,1)}, u32[]{:S(2)}) copy-start(bf16[1536,256]{1,0:T(8,128)(2,1)} %param.9) | copy-start | bytes 2359300
  9.5 27.4 %all-to-all-start = ((bf16[192,8,192]{0,2,1:T(8,128)(2,1)}), bf16[192,8,192]{0,2,1:T(8,128)(2,1)S(1)}, u32[]{:S(2)}, u32[]{:S(2)}) async-start(bf16[192,8,192]{0,2,1:T(8,128)(2,1)} %bitcast), calls=%async_computation | async-start | bytes 1572864 | tf_op jit(solution)/shard_map/all_to_all | solution.py:75
  16.9 60.9 %reduce-scatter.13.cloned.1.call-start = ((), (), s32[]{:S(2)}) async-start(), calls=%async_computation.12 | async-start | bytes 1769472 | tf_op jit(solution)/shard_map/reduce_scatter | solution.py:58
  40.0 173.5 %all-gather.9.cloned.1.call-start = ((), (), s32[]{:S(2)}) async-start(), calls=%async_computation.8 | async-start | bytes 6488064 | tf_op jit(solution)/shard_map/all_gather | solution.py:13
  77.8 404.7 %all-reduce.5.cloned.1.call-start = ((), (), s32[]{:S(2)}) async-start(), calls=%async_computation.5 | async-start | bytes 524288 | tf_op jit(solution)/shard_map/psum | solution.py:53
  235.9 349.0 %reduce-scatter.15.cloned.1.call-start = ((), (), s32[]{:S(2)}) async-start(), calls=%async_computation.13 | async-start | bytes 1769472 | tf_op jit(solution)/shard_map/reduce_scatter | solution.py:58
  547.6 172.8 %all-gather.11.cloned.1.call-start = ((), (), s32[]{:S(2)}) async-start(), calls=%async_computation.9 | async-start | bytes 6488064 | tf_op jit(solution)/shard_map/all_gather | solution.py:13
  584.9 404.6 %all-reduce.7.cloned.1.call-start = ((), (), s32[]{:S(2)}) async-start(), calls=%async_computation.6 | async-start | bytes 524288 | tf_op jit(solution)/shard_map/psum | solution.py:53
  742.7 349.5 %reduce-scatter.17.cloned.1.call-start = ((), (), s32[]{:S(2)}) async-start(), calls=%async_computation.14 | async-start | bytes 1769472 | tf_op jit(solution)/shard_map/reduce_scatter | solution.py:58
  1054.9 172.9 %all-gather.13.cloned.1.call-start = ((), (), s32[]{:S(2)}) async-start(), calls=%async_computation.10 | async-start | bytes 6488064 | tf_op jit(solution)/shard_map/all_gather | solution.py:13
  1092.2 404.8 %all-reduce.9.cloned.1.call-start = ((), (), s32[]{:S(2)}) async-start(), calls=%async_computation.7 | async-start | bytes 524288 | tf_op jit(solution)/shard_map/psum | solution.py:53
  1250.2 349.3 %reduce-scatter.19.cloned.1.call-start = ((), (), s32[]{:S(2)}) async-start(), calls=%async_computation.15 | async-start | bytes 1769472 | tf_op jit(solution)/shard_map/reduce_scatter | solution.py:58
  1560.2 2.0 copy-start.1
  1562.3 172.9 %all-gather.15.cloned.1.call-start = ((), (), s32[]{:S(2)}) async-start(), calls=%async_computation.11 | async-start | bytes 6488064 | tf_op jit(solution)/shard_map/all_gather | solution.py:13
  1755.8 0.7 copy-start.3
  1756.2 5.9 copy-start.2
Sparse Core Ops, SparseCore 0:
  40.1 37.5 reduce-scatter.12
  81.1 132.3 all-gather.8
  236.0 246.4 all-reduce.4
  547.7 37.0 reduce-scatter.14
  588.1 132.2 all-gather.10
  742.8 246.6 all-reduce.6
  1055.1 37.0 reduce-scatter.16
  1095.6 132.2 all-gather.12
  1250.3 246.6 all-reduce.8
  1562.4 37.0 reduce-scatter.18
  1602.9 132.2 all-gather.14
